TPU v7x, 512 devices: a whole 4x8x8 slice. The times are simulated.
512 devices in a mesh: doc: 32 (over z_hi, y, core), lab: 16 (over z_lo, x).
Axes of the slice: x: 4, y: 8, z: 8 (z_hi: 2, z_lo: 4; z = z_hi * 4 + z_lo), core: 2. Of those that a mesh axis runs over, the one named last changes fastest.
Arguments:
- embeddings: bfloat16 [262144, 768], P(('doc', 'lab')), may hold values from -6 to 6
- positives: int32 [262144, 16], P(('doc', 'lab')), may hold values from 0 to 16383, as said below
- weights: float32 [131072, 768], P(('doc', 'lab')), may hold values from -6 to 6
- parents: int32 [131072], replicated, may hold values from 0 to 254, as said below
- owners: int32 [4, 32], replicated, may hold values from 0 to 15
- shortlist: int32 [4, 512, 4], replicated, may hold values from 0 to 3, as said below
- counts: int32 [4, 512], replicated, may hold values from 1 to 4, as said below
Outputs:
- trained: float32 [131072, 768], P(('doc', 'lab'))
- momentum: float32 [131072, 768], P(('doc', 'lab'))
Inputs may be any that keep to these rules, and one draw needn't show every extreme that they name: `positives`: each positive code is (s * 16 + j) * 256 + l with s < 4, j < 16, l < 256; repeats allowed. parents[l] is a row of l's own block below l's row; row 0 of a block is its own parent. `shortlist`: the 4 tile numbers of one step and block are distinct. `counts`: in every step some block has all 4 slots live.
All inputs are finite; a program needn't handle non-finite values.
Results may differ from a plain program's by a relative error of at most 0.0003.
Values may be sent and summed in bfloat16 or wider, within the bound.
A program may use at most 64 MiB of HBM per device.

v0:
```python
import jax
import jax.numpy as jnp
from jax import lax
from jax.sharding import PartitionSpec as P

TILE = 128
STEPS = 4
learning_rate = 0.1
beta_rate = 0.9
pull_rate = 1.0


def from_root(value, axis, source):
    kept = jnp.where(lax.axis_index(axis) == source, value, 0).astype(value.dtype)
    return lax.psum(kept, axis)


def from_behind(value, axis, by):
    length = lax.axis_size(axis)
    return lax.ppermute(value, axis, [(i, (i + by) % length) for i in range(length)])


def pick_rows(panel, labels, tiles, tile_rows):
    width = panel.shape[1]
    shaped = panel.reshape(panel.shape[0] // tile_rows, tile_rows, width)
    lshaped = labels.reshape(labels.shape[0] // tile_rows, tile_rows, labels.shape[1])
    rows = jnp.take(shaped, tiles, axis=0).reshape(tiles.shape[0] * tile_rows, width)
    picked = jnp.take(lshaped, tiles, axis=0).reshape(tiles.shape[0] * tile_rows, labels.shape[1])
    return (rows, picked)


def block_update(weight, moment, rows, picked, base, parent_rows, live):
    scale = 1.0 / jnp.sqrt(jnp.float32(rows.shape[1]))
    rows32 = rows.astype(jnp.float32)
    scores = (
        jnp.dot(
            rows32, weight.T, precision=lax.Precision.HIGHEST, preferred_element_type=jnp.float32
        )
        * scale
    )
    label_ids = base + jnp.arange(weight.shape[0], dtype=jnp.int32)
    target = jnp.any(picked[:, :, None] == label_ids[None, None, :], axis=1).astype(jnp.float32)
    resid = (jax.nn.sigmoid(scores) - target) * live[:, None]
    grad = (
        jnp.dot(
            resid.T, rows32, precision=lax.Precision.HIGHEST, preferred_element_type=jnp.float32
        )
        * scale
    )
    grad = grad + pull_rate * (weight - jnp.take(weight, parent_rows, axis=0))
    moment = beta_rate * moment + grad
    return (weight - learning_rate * moment, moment)


def local(embeddings, positives, weights, parents, owners, shortlist, counts):
    doc_index = lax.axis_index("doc")
    lab_index = lax.axis_index("lab")
    doc_count = lax.axis_size("doc")
    lab_count = lax.axis_size("lab")
    block_rows = weights.shape[0]
    tile_rows = TILE
    slots = shortlist.shape[2]
    slot_of_row = jnp.arange(slots * tile_rows, dtype=jnp.int32) // tile_rows
    weight = weights
    moment = jnp.zeros_like(weights)
    for step in range(STEPS):
        root = owners[step, doc_index]
        panel = from_root(embeddings, "lab", root)
        labels = from_root(positives, "lab", root)
        met_block = (doc_index - step) % doc_count * lab_count + lab_index
        if step > 0:
            weight, moment = from_behind((weight, moment), "doc", 1)
        tiles = lax.dynamic_index_in_dim(shortlist[step], met_block, 0, keepdims=False)
        rows, picked = pick_rows(panel, labels, tiles, tile_rows)
        live = (slot_of_row < counts[step, met_block]).astype(jnp.float32)
        parent_rows = lax.dynamic_slice_in_dim(parents, met_block * block_rows, block_rows, 0)
        code_base = (step * lab_count + lab_index) * block_rows
        weight, moment = block_update(weight, moment, rows, picked, code_base, parent_rows, live)
    weight, moment = from_behind((weight, moment), "doc", -(STEPS - 1))
    return (weight, moment)


def solution(mesh):
    return jax.shard_map(
        local,
        mesh=mesh,
        in_specs=(
            P(("doc", "lab"), None),
            P(("doc", "lab"), None),
            P(("doc", "lab"), None),
            P(),
            P(),
            P(),
            P(),
        ),
        out_specs=(P(("doc", "lab"), None), P(("doc", "lab"), None)),
        check_vma=False,
    )
```

profile of v0, /device:TPU:55, one launch (start us, length us, event | category | flops | bytes accessed | tf_op | source)
XLA Modules:
  0.0 590.3 jit_solution(14270951001734933305)
XLA Ops:
  7.2 1.5 constant_dynamic-slice_fusion.5
  11.3 0.8 select_bitcast_fusion
  12.0 0.6 copy_bitcast_fusion
  12.7 0.6 copy_bitcast_fusion.2
  13.4 2.9 broadcast_select_fusion.4
  16.3 0.6 copy-done.6
  17.0 0.2 dynamic-slice_reduce_fusion.3
  17.2 0.2 dynamic-slice_reduce_fusion.2
  17.4 0.8 compare_and_fusion
  18.2 1.1 gather_fusion.2
  19.3 0.2 dynamic-slice_reduce_fusion.1
  19.5 0.2 dynamic-slice_reduce_fusion
  19.7 1.5 constant_dynamic-slice_fusion.4
  21.2 0.6 fusion.37
  21.8 0.6 fusion.38
  22.5 0.6 fusion.39
  23.1 0.6 fusion.40
  23.9 144.6 %all-reduce.5.cloned.1.call-done = (s32[4,128,16]{1,2,0:T(8,128)}, s32[4,128,16]{1,2,0:T(8,128)}, s32[4,128,16]{1,2,0:T(8,128)}, s32[4,128,16]{1,2,0:T(8,128)}) async-done(((s32[4,128,16]{1,2,0:T(8,128)}, s32[4,128,16]{1,2,0:T(8,128)}, s32[4,128,16]{1,2,0:T(8,128)}, s32[4,128,16]{1,2,0:T(8,128)}), (s32[4,128,16]{1,2,0:T(8,128)}, s32[4,128,16]{1,2,0:T(8,128)}, s32[4,128,16]{1,2,0:T(8,128)}, ...) | async-done | bytes 131088 | tf_op jit(solution)/shard_map/psum | solution.py:15
  168.5 1.3 gather_fusion.1
  170.1 5.9 compare_reduce_fusion.3
  175.9 175.2 %all-reduce.7.cloned.1.call-done = (bf16[4,128,768]{2,1,0:T(8,128)(2,1)}, bf16[4,128,768]{2,1,0:T(8,128)(2,1)}, bf16[4,128,768]{2,1,0:T(8,128)(2,1)}, bf16[4,128,768]{2,1,0:T(8,128)(2,1)}) async-done(((bf16[4,128,768]{2,1,0:T(8,128)(2,1)}, bf16[4,128,768]{2,1,0:T(8,128)(2,1)}, bf16[4,128,768]{2,1,0:T(8,128)(2,1)}, bf16[4,128,768]{2,1,0:T(8,128)(2,1)}), (bf16[4,128,768]{2,1,0:T(8,128)(2,1)}, ...) | async-done | bytes 3145744 | tf_op jit(solution)/shard_map/psum | solution.py:15
  351.1 1.7 gather_fusion
  352.9 0.1 broadcast_select_fusion.3
  353.0 0.9 fusion.24
  354.0 1.8 multiply_subtract_fusion.3
  355.8 12.5 %collective-permute-start = (f32[256,768]{1,0:T(8,128)}, f32[256,768]{1,0:T(8,128)S(1)}, u32[]{:S(2)}, u32[]{:S(2)}) collective-permute-start(f32[256,768]{1,0:T(8,128)} %get-tuple-element.53), channel_id=1, source_target_pairs={{0,16},{16,32},{32,48},{48,64},{64,80},{80,96},{96,112},{112,128},... | collective-permute-start | bytes 2359304 | tf_op jit(solution)/shard_map/ppermute | solution.py:20
  368.4 0.6 gather_fusion.4
  369.1 5.9 compare_reduce_fusion.2
  375.0 1.7 gather_fusion.3
  376.8 1.9 collective-permute-start.1
  378.7 0.1 broadcast_select_fusion.2
  378.9 1.1 gather_fusion.5
  380.0 0.9 fusion.22
  380.9 0.9 convolution_multiply_fusion.2
  381.8 5.8 collective-permute-done.1
  387.6 2.3 multiply_subtract_fusion.2
  389.9 4.6 collective-permute-start.2
  394.6 0.6 gather_fusion.7
  395.4 5.9 compare_reduce_fusion.1
  401.3 0.6 gather_fusion.6
  401.9 15.6 %collective-permute-start.3 = (f32[256,768]{1,0:T(8,128)S(1)}, f32[256,768]{1,0:T(8,128)}, u32[]{:S(2)}, u32[]{:S(2)}) collective-permute-start(f32[256,768]{1,0:T(8,128)S(1)} %get-tuple-element.22), channel_id=1, source_target_pairs={{0,16},{16,32},{32,48},{48,64},{64,80},{80,96},{96,112},{112,128},... | collective-permute-start | bytes 2359304 | tf_op jit(solution)/shard_map/ppermute | solution.py:20
  417.5 0.1 broadcast_select_fusion.1
  417.6 1.1 gather_fusion.8
  418.7 0.9 fusion.20
  419.7 0.9 convolution_multiply_fusion.1
  420.6 5.6 collective-permute-done.3
  426.2 2.3 multiply_subtract_fusion.1
  428.5 7.3 %collective-permute-start.4 = (f32[256,768]{1,0:T(8,128)}, f32[256,768]{1,0:T(8,128)S(1)}, u32[]{:S(2)}, u32[]{:S(2)}) collective-permute-start(f32[256,768]{1,0:T(8,128)} %get-tuple-element.17), channel_id=1, source_target_pairs={{0,16},{16,32},{32,48},{48,64},{64,80},{80,96},{96,112},{112,128},... | collective-permute-start | bytes 2359304 | tf_op jit(solution)/shard_map/ppermute | solution.py:20
  435.9 0.6 gather_fusion.10
  436.7 5.9 compare_reduce_fusion
  442.6 0.6 gather_fusion.9
  443.2 22.2 %collective-permute-start.5 = (f32[256,768]{1,0:T(8,128)S(1)}, f32[256,768]{1,0:T(8,128)}, u32[]{:S(2)}, u32[]{:S(2)}) collective-permute-start(f32[256,768]{1,0:T(8,128)S(1)} %get-tuple-element.18), channel_id=1, source_target_pairs={{0,16},{16,32},{32,48},{48,64},{64,80},{80,96},{96,112},{112,128},... | collective-permute-start | bytes 2359304 | tf_op jit(solution)/shard_map/ppermute | solution.py:20
  465.4 0.1 broadcast_select_fusion
  465.6 1.1 gather_fusion.11
  466.7 0.9 fusion.18
  467.6 0.9 convolution_multiply_fusion
  468.5 5.8 collective-permute-done.5
  474.3 1.4 multiply_subtract_fusion
  475.8 1.9 collective-permute-start.6
  477.7 1.9 collective-permute-start.7
  479.6 87.9 %collective-permute-done.6 = f32[256,768]{1,0:T(8,128)S(1)} collective-permute-done((f32[256,768]{1,0:T(8,128)S(1)}, f32[256,768]{1,0:T(8,128)S(1)}, u32[]{:S(2)}, u32[]{:S(2)}) %collective-permute-start.6) | collective-permute-done | bytes 786464 | tf_op jit(solution)/shard_map/ppermute | solution.py:20
  567.5 14.3 %collective-permute-done.7 = f32[256,768]{1,0:T(8,128)S(1)} collective-permute-done((f32[256,768]{1,0:T(8,128)S(1)}, f32[256,768]{1,0:T(8,128)S(1)}, u32[]{:S(2)}, u32[]{:S(2)}) %collective-permute-start.7) | collective-permute-done | bytes 786464 | tf_op jit(solution)/shard_map/ppermute | solution.py:20
  581.7 0.9 copy.63
  582.6 0.9 copy.64
  (45 shorter events, 1.0 us)
Async XLA Ops:
  7.2 161.4 %all-reduce.5.cloned.1.call-start = ((), (), s32[]{:S(2)}) async-start(), calls=%async_computation | async-start | bytes 262144 | tf_op jit(solution)/shard_map/psum | solution.py:15
  13.3 337.8 %all-reduce.7.cloned.1.call-start = ((), (), s32[]{:S(2)}) async-start(), calls=%async_computation.1 | async-start | bytes 6291456 | tf_op jit(solution)/shard_map/psum | solution.py:15
  16.2 0.8 copy-start.6
  16.2 2.0 copy-start
  354.0 14.4 %copy-start.3 = (s32[4,128,16]{1,2,0:T(8,128)S(1)}, s32[4,128,16]{1,2,0:T(8,128)}, u32[]{:S(2)}) copy-start(s32[4,128,16]{1,2,0:T(8,128)} %get-tuple-element.6) | copy-start | bytes 98308
  355.8 23.0 %collective-permute-start = (f32[256,768]{1,0:T(8,128)}, f32[256,768]{1,0:T(8,128)S(1)}, u32[]{:S(2)}, u32[]{:S(2)}) collective-permute-start(f32[256,768]{1,0:T(8,128)} %get-tuple-element.53), channel_id=1, source_target_pairs={{0,16},{16,32},{32,48},{48,64},{64,80},{80,96},{96,112},{112,128},... | collective-permute-start | bytes 2359304 | tf_op jit(solution)/shard_map/ppermute | solution.py:20
  376.8 10.8 %collective-permute-start.1 = (f32[256,768]{1,0:T(8,128)S(1)}, f32[256,768]{1,0:T(8,128)}, u32[]{:S(2)}, u32[]{:S(2)}) collective-permute-start(f32[256,768]{1,0:T(8,128)S(1)} %get-tuple-element.54), channel_id=1, source_target_pairs={{0,16},{16,32},{32,48},{48,64},{64,80},{80,96},{96,112},{112,128},... | collective-permute-start | bytes 2359304 | tf_op jit(solution)/shard_map/ppermute | solution.py:20
  387.6 7.0 %copy-start.2 = (s32[4,128,16]{1,2,0:T(8,128)S(1)}, s32[4,128,16]{1,2,0:T(8,128)}, u32[]{:S(2)}) copy-start(s32[4,128,16]{1,2,0:T(8,128)} %get-tuple-element.7) | copy-start | bytes 98308
  389.9 11.3 %copy-start.5 = (bf16[4,128,768]{2,1,0:T(8,128)(2,1)S(1)}, bf16[4,128,768]{2,1,0:T(8,128)(2,1)}, u32[]{:S(2)}) copy-start(bf16[4,128,768]{2,1,0:T(8,128)(2,1)} %get-tuple-element.11) | copy-start | bytes 2359300
  389.9 27.7 %collective-permute-start.2 = (f32[256,768]{1,0:T(8,128)}, f32[256,768]{1,0:T(8,128)S(1)}, u32[]{:S(2)}, u32[]{:S(2)}) collective-permute-start(f32[256,768]{1,0:T(8,128)} %get-tuple-element.21), channel_id=1, source_target_pairs={{0,16},{16,32},{32,48},{48,64},{64,80},{80,96},{96,112},{112,128},... | collective-permute-start | bytes 2359304 | tf_op jit(solution)/shard_map/ppermute | solution.py:20
  401.9 24.3 %collective-permute-start.3 = (f32[256,768]{1,0:T(8,128)S(1)}, f32[256,768]{1,0:T(8,128)}, u32[]{:S(2)}, u32[]{:S(2)}) collective-permute-start(f32[256,768]{1,0:T(8,128)S(1)} %get-tuple-element.22), channel_id=1, source_target_pairs={{0,16},{16,32},{32,48},{48,64},{64,80},{80,96},{96,112},{112,128},... | collective-permute-start | bytes 2359304 | tf_op jit(solution)/shard_map/ppermute | solution.py:20
  426.2 9.7 %copy-start.1 = (s32[4,128,16]{1,2,0:T(8,128)S(1)}, s32[4,128,16]{1,2,0:T(8,128)}, u32[]{:S(2)}) copy-start(s32[4,128,16]{1,2,0:T(8,128)} %get-tuple-element.8) | copy-start | bytes 98308
  428.5 14.0 %copy-start.4 = (bf16[4,128,768]{2,1,0:T(8,128)(2,1)S(1)}, bf16[4,128,768]{2,1,0:T(8,128)(2,1)}, u32[]{:S(2)}) copy-start(bf16[4,128,768]{2,1,0:T(8,128)(2,1)} %get-tuple-element.12) | copy-start | bytes 2359300
  428.5 37.0 %collective-permute-start.4 = (f32[256,768]{1,0:T(8,128)}, f32[256,768]{1,0:T(8,128)S(1)}, u32[]{:S(2)}, u32[]{:S(2)}) collective-permute-start(f32[256,768]{1,0:T(8,128)} %get-tuple-element.17), channel_id=1, source_target_pairs={{0,16},{16,32},{32,48},{48,64},{64,80},{80,96},{96,112},{112,128},... | collective-permute-start | bytes 2359304 | tf_op jit(solution)/shard_map/ppermute | solution.py:20
  443.2 31.1 %collective-permute-start.5 = (f32[256,768]{1,0:T(8,128)S(1)}, f32[256,768]{1,0:T(8,128)}, u32[]{:S(2)}, u32[]{:S(2)}) collective-permute-start(f32[256,768]{1,0:T(8,128)S(1)} %get-tuple-element.18), channel_id=1, source_target_pairs={{0,16},{16,32},{32,48},{48,64},{64,80},{80,96},{96,112},{112,128},... | collective-permute-start | bytes 2359304 | tf_op jit(solution)/shard_map/ppermute | solution.py:20
  475.8 91.7 %collective-permute-start.6 = (f32[256,768]{1,0:T(8,128)S(1)}, f32[256,768]{1,0:T(8,128)S(1)}, u32[]{:S(2)}, u32[]{:S(2)}) collective-permute-start(f32[256,768]{1,0:T(8,128)S(1)} %get-tuple-element.13), channel_id=1, source_target_pairs={{0,464},{16,480},{32,496},{48,0},{64,16},{80,32},{96,48},{112,64},... | collective-permute-start | bytes 2359304 | tf_op jit(solution)/shard_map/ppermute | solution.py:20
  477.7 104.1 %collective-permute-start.7 = (f32[256,768]{1,0:T(8,128)S(1)}, f32[256,768]{1,0:T(8,128)S(1)}, u32[]{:S(2)}, u32[]{:S(2)}) collective-permute-start(f32[256,768]{1,0:T(8,128)S(1)} %get-tuple-element.14), channel_id=1, source_target_pairs={{0,464},{16,480},{32,496},{48,0},{64,16},{80,32},{96,48},{112,64},... | collective-permute-start | bytes 2359304 | tf_op jit(solution)/shard_map/ppermute | solution.py:20
Sparse Core Ops, SparseCore 0:
  13.4 155.0 all-reduce.4
  172.6 178.4 all-reduce.6
where the time goes:
time: 591 us; the launch traced here: 590 us
  waiting for transfers between devices  439 us (74%)
  starting transfers between devices  68.1 us (12%)
  other arithmetic  37.6 us (6%)
  local copies, waits for them, and re-layouts  19.8 us (3%)
  between operations  17.3 us (3%)
  matrix products  8.22 us (1%)
    psum x2, waiting for transfers between devices, from_root(): return lax.psum(kept, axis)  320 us
    ppermute x8, waiting for transfers between devices, from_behind(): lax.ppermute(value, axis, [(i, (i + by) % length) for i in range(length)])  119 us
    ppermute x8, starting transfers between devices, from_behind(): lax.ppermute(value, axis, [(i, (i + by) % length) for i in range(length)])  68 us
    reduce_or x4, other arithmetic, block_update(): jnp.any(picked[:, :, None] == label_ids[None, None, :], axis=1)  23.6 us
  transfers between devices with their start and end apart: 10, of which 7 were waited for; matrix products, arithmetic and copies ran while one was open for 8% of the time, Pallas kernels for 0%

commit v1 on v0

--- a/solution.py
+++ b/solution.py
@@ -10,9 +10,15 @@
 pull_rate = 1.0
 
 
+def trace_sample(vec, row_axis):
+    x_new = lax.all_gather(vec, row_axis)
+    new = jnp.sum(x_new, 0)
+    return new
+
+
 def from_root(value, axis, source):
     kept = jnp.where(lax.axis_index(axis) == source, value, 0).astype(value.dtype)
-    return lax.psum(kept, axis)
+    return trace_sample(kept, axis)
 
 
 def from_behind(value, axis, by):

time: 591 us -> 819 us (1.39)
  blocking collectives: 0 us -> 162 us
  waiting for transfers between devices: 439 us -> 502 us
  other arithmetic: 37.6 us -> 66.2 us
  starting transfers between devices: 68.1 us -> 46 us
    all_gather x0 -> x4, waiting for transfers between devices: none -> 369 us  [trace_sample(): x_new = lax.all_gather(vec, row_axis)]
    psum x2 -> x0, waiting for transfers between devices: 320 us -> none  [from_root(): return lax.psum(kept, axis)]
    all_gather x0 -> x4, blocking collectives: none -> 162 us  [trace_sample(): x_new = lax.all_gather(vec, row_axis)]
    reduce_sum x0 -> x8, other arithmetic: none -> 27.7 us  [trace_sample(): new = jnp.sum(x_new, 0)]
    ppermute x8, starting transfers between devices: 68 us -> 45.8 us  [from_behind(): lax.ppermute(value, axis, [(i, (i + by) % length) for i in range(length)])]
    ppermute x8, waiting for transfers between devices: 119 us -> 131 us  [from_behind(): lax.ppermute(value, axis, [(i, (i + by) % length) for i in range(length)])]
  transfers between devices with their start and end apart: 10 -> 12, of which waited for: 7 -> 8; matrix products, arithmetic and copies ran while one was open for 8% -> 10% of each run, Pallas kernels for 0% -> 0%
where the time goes in v1:
time: 819 us; the launch traced here: 818 us
  waiting for transfers between devices  502 us (61%)
  blocking collectives  162 us (20%)
  other arithmetic  66.2 us (8%)
  starting transfers between devices  46 us (6%)
  between operations  17.1 us (2%)
  local copies, waits for them, and re-layouts  16.9 us (2%)
  matrix products  8.24 us (1%)
    all_gather x4, waiting for transfers between devices, trace_sample(): x_new = lax.all_gather(vec, row_axis)  369 us
    all_gather x4, blocking collectives, trace_sample(): x_new = lax.all_gather(vec, row_axis)  162 us
    ppermute x8, waiting for transfers between devices, from_behind(): lax.ppermute(value, axis, [(i, (i + by) % length) for i in range(length)])  131 us
    ppermute x8, starting transfers between devices, from_behind(): lax.ppermute(value, axis, [(i, (i + by) % length) for i in range(length)])  45.8 us
    reduce_sum x8, other arithmetic, trace_sample(): new = jnp.sum(x_new, 0)  27.7 us
    reduce_or x4, other arithmetic, block_update(): jnp.any(picked[:, :, None] == label_ids[None, None, :], axis=1)  24.5 us
  transfers between devices with their start and end apart: 12, of which 8 were waited for; matrix products, arithmetic and copies ran while one was open for 10% of the time, Pallas kernels for 0%

profile of v1, /device:TPU:55, one launch (start us, length us, event | category | flops | bytes accessed | tf_op | source)
XLA Modules:
  0.0 818.4 jit_solution(11423930810545539306)
XLA Ops:
  7.2 1.5 constant_dynamic-slice_fusion.5
  11.3 2.9 broadcast_select_fusion.4
  14.2 0.7 all-gather.15.cloned.1.call-update
  15.0 0.7 all-gather.17.cloned.1.call-update
  16.4 0.8 broadcast_select_fusion.12
  17.1 37.2 %all-gather.1 = s32[8192,16]{0,1:T(8,128)S(1)} all-gather(s32[512,16]{0,1:T(8,128)S(1)} %get-tuple-element.31), channel_id=3, replica_groups=mesh['doc'=32,'lab'=16] {'lab'}, dimensions={0}, use_global_device_ids=true | all-gather | bytes 557056 | tf_op jit(solution)/shard_map/all_gather | solution.py:14
  55.2 0.6 gather_fusion.1
  55.8 0.8 copy.37
  56.6 46.3 %all-gather.3 = s32[8192,16]{0,1:T(8,128)S(1)} all-gather(s32[512,16]{0,1:T(8,128)S(1)} %get-tuple-element.30), channel_id=5, replica_groups=mesh['doc'=32,'lab'=16] {'lab'}, dimensions={0}, use_global_device_ids=true | all-gather | bytes 557056 | tf_op jit(solution)/shard_map/all_gather | solution.py:14
  103.2 39.3 %all-gather.5 = s32[8192,16]{0,1:T(8,128)S(1)} all-gather(s32[512,16]{0,1:T(8,128)S(1)} %get-tuple-element.32), channel_id=7, replica_groups=mesh['doc'=32,'lab'=16] {'lab'}, dimensions={0}, use_global_device_ids=true | all-gather | bytes 557056 | tf_op jit(solution)/shard_map/all_gather | solution.py:14
  142.8 39.3 %all-gather.7 = s32[8192,16]{0,1:T(8,128)S(1)} all-gather(s32[512,16]{0,1:T(8,128)S(1)} %get-tuple-element.29), channel_id=9, replica_groups=mesh['doc'=32,'lab'=16] {'lab'}, dimensions={0}, use_global_device_ids=true | all-gather | bytes 557056 | tf_op jit(solution)/shard_map/all_gather | solution.py:14
  182.5 0.8 compare_and_fusion
  183.3 1.1 gather_fusion.2
  184.5 0.6 gather_fusion.4
  185.5 1.5 constant_dynamic-slice_fusion.4
  187.0 0.7 fusion.37
  187.7 0.6 fusion.38
  188.3 0.6 fusion.39
  189.3 6.8 compare_reduce_fusion.3
  196.2 7.0 reduce_sum.84
  203.2 0.6 gather_fusion
  204.0 0.9 fusion.24
  204.9 1.9 multiply_subtract_fusion.3
  206.8 19.7 %collective-permute-start = (f32[256,768]{1,0:T(8,128)}, f32[256,768]{1,0:T(8,128)S(1)}, u32[]{:S(2)}, u32[]{:S(2)}) collective-permute-start(f32[256,768]{1,0:T(8,128)} %get-tuple-element.45), channel_id=1, source_target_pairs={{0,16},{16,32},{32,48},{48,64},{64,80},{80,96},{96,112},{112,128},... | collective-permute-start | bytes 2359304 | tf_op jit(solution)/shard_map/ppermute | solution.py:26
  227.3 5.9 compare_reduce_fusion.2
  233.2 92.7 %all-gather.15.cloned.1.call-done = bf16[8192,768]{1,0:T(8,128)(2,1)} async-done(((bf16[512,768]{1,0:T(8,128)(2,1)}), bf16[8192,768]{1,0:T(8,128)(2,1)}) %all-gather.15.cloned.1.call-update) | async-done | bytes 12582928 | tf_op jit(solution)/shard_map/all_gather | solution.py:14
  325.9 6.8 reduce_sum.86
  332.7 0.6 gather_fusion.3
  333.3 2.8 collective-permute-start.1
  336.2 1.1 gather_fusion.5
  337.3 0.9 fusion.22
  338.3 0.9 convolution_multiply_fusion.2
  339.2 5.8 collective-permute-done.1
  345.0 2.3 multiply_subtract_fusion.2
  347.3 4.5 collective-permute-start.2
  351.9 0.6 gather_fusion.10
  352.6 5.9 compare_reduce_fusion.1
  358.5 130.9 %all-gather.17.cloned.1.call-done = bf16[8192,768]{1,0:T(8,128)(2,1)} async-done(((bf16[512,768]{1,0:T(8,128)(2,1)}), bf16[8192,768]{1,0:T(8,128)(2,1)}) %all-gather.17.cloned.1.call-update) | async-done | bytes 12582928 | tf_op jit(solution)/shard_map/all_gather | solution.py:14
  489.3 6.8 reduce_sum.88
  496.1 0.6 gather_fusion.6
  496.7 3.1 collective-permute-start.3
  499.9 1.1 gather_fusion.8
  501.0 0.9 fusion.20
  502.0 0.9 convolution_multiply_fusion.1
  502.8 5.6 collective-permute-done.3
  508.5 2.3 multiply_subtract_fusion.1
  510.8 4.5 collective-permute-start.4
  515.4 0.6 fusion.40
  516.0 5.9 compare_reduce_fusion
  521.9 145.5 %all-gather.19.cloned.1.call-done = bf16[8192,768]{1,0:T(8,128)(2,1)} async-done(((bf16[512,768]{1,0:T(8,128)(2,1)}), bf16[8192,768]{1,0:T(8,128)(2,1)}) %all-gather.19.cloned.1.call-update) | async-done | bytes 12582928 | tf_op jit(solution)/shard_map/all_gather | solution.py:14
  667.4 6.8 reduce_sum.90
  674.2 0.6 gather_fusion.9
  674.8 2.8 collective-permute-start.5
  677.8 1.1 gather_fusion.11
  678.9 0.9 fusion.18
  679.8 0.9 convolution_multiply_fusion
  680.7 5.8 collective-permute-done.5
  686.5 1.4 multiply_subtract_fusion
  688.0 5.3 collective-permute-start.6
  693.3 3.2 collective-permute-start.7
  696.5 99.6 %collective-permute-done.6 = f32[256,768]{1,0:T(8,128)S(1)} collective-permute-done((f32[256,768]{1,0:T(8,128)S(1)}, f32[256,768]{1,0:T(8,128)S(1)}, u32[]{:S(2)}, u32[]{:S(2)}) %collective-permute-start.6) | collective-permute-done | bytes 786464 | tf_op jit(solution)/shard_map/ppermute | solution.py:26
  796.1 14.0 %collective-permute-done.7 = f32[256,768]{1,0:T(8,128)S(1)} collective-permute-done((f32[256,768]{1,0:T(8,128)S(1)}, f32[256,768]{1,0:T(8,128)S(1)}, u32[]{:S(2)}, u32[]{:S(2)}) %collective-permute-start.7) | collective-permute-done | bytes 786464 | tf_op jit(solution)/shard_map/ppermute | solution.py:26
  810.1 0.9 copy.59
  811.0 0.9 copy.60
  (61 shorter events, 4.9 us)
Async XLA Ops:
  7.2 47.5 %copy-start.1 = (s32[4,512,4]{1,2,0:T(4,128)S(1)}, s32[4,512,4]{1,2,0:T(4,128)}, u32[]{:S(2)}) copy-start(s32[4,512,4]{1,2,0:T(4,128)} %param.18) | copy-start | bytes 98308
  7.2 176.1 %copy-start = (f32[256,768]{1,0:T(8,128)S(1)}, f32[256,768]{1,0:T(8,128)}, u32[]{:S(2)}) copy-start(f32[256,768]{1,0:T(8,128)} %param.15) | copy-start | bytes 2359300
  7.2 189.0 %all-gather.13.cloned.1.call-start = ((), (), s32[]{:S(2)}) async-start(), calls=%async_computation | async-start | bytes 13369344 | tf_op jit(solution)/shard_map/all_gather | solution.py:14
  14.2 311.7 %all-gather.15.cloned.1.call-start = ((), (), s32[]{:S(2)}) async-start(), calls=%async_computation.1 | async-start | bytes 13369344 | tf_op jit(solution)/shard_map/all_gather | solution.py:14
  14.9 474.4 %all-gather.17.cloned.1.call-start = ((), (), s32[]{:S(2)}) async-start(), calls=%async_computation.2 | async-start | bytes 13369344 | tf_op jit(solution)/shard_map/all_gather | solution.py:14
  15.7 651.8 %all-gather.19.cloned.1.call-start = ((), (), s32[]{:S(2)}) async-start(), calls=%async_computation.3 | async-start | bytes 13369344 | tf_op jit(solution)/shard_map/all_gather | solution.py:14
  206.8 129.5 %collective-permute-start = (f32[256,768]{1,0:T(8,128)}, f32[256,768]{1,0:T(8,128)S(1)}, u32[]{:S(2)}, u32[]{:S(2)}) collective-permute-start(f32[256,768]{1,0:T(8,128)} %get-tuple-element.45), channel_id=1, source_target_pairs={{0,16},{16,32},{32,48},{48,64},{64,80},{80,96},{96,112},{112,128},... | collective-permute-start | bytes 2359304 | tf_op jit(solution)/shard_map/ppermute | solution.py:26
  333.3 11.7 %collective-permute-start.1 = (f32[256,768]{1,0:T(8,128)S(1)}, f32[256,768]{1,0:T(8,128)}, u32[]{:S(2)}, u32[]{:S(2)}) collective-permute-start(f32[256,768]{1,0:T(8,128)S(1)} %get-tuple-element.46), channel_id=1, source_target_pairs={{0,16},{16,32},{32,48},{48,64},{64,80},{80,96},{96,112},{112,128},... | collective-permute-start | bytes 2359304 | tf_op jit(solution)/shard_map/ppermute | solution.py:26
  347.3 152.6 %collective-permute-start.2 = (f32[256,768]{1,0:T(8,128)}, f32[256,768]{1,0:T(8,128)S(1)}, u32[]{:S(2)}, u32[]{:S(2)}) collective-permute-start(f32[256,768]{1,0:T(8,128)} %get-tuple-element.13), channel_id=1, source_target_pairs={{0,16},{16,32},{32,48},{48,64},{64,80},{80,96},{96,112},{112,128},... | collective-permute-start | bytes 2359304 | tf_op jit(solution)/shard_map/ppermute | solution.py:26
  496.7 11.8 %collective-permute-start.3 = (f32[256,768]{1,0:T(8,128)S(1)}, f32[256,768]{1,0:T(8,128)}, u32[]{:S(2)}, u32[]{:S(2)}) collective-permute-start(f32[256,768]{1,0:T(8,128)S(1)} %get-tuple-element.14), channel_id=1, source_target_pairs={{0,16},{16,32},{32,48},{48,64},{64,80},{80,96},{96,112},{112,128},... | collective-permute-start | bytes 2359304 | tf_op jit(solution)/shard_map/ppermute | solution.py:26
  510.8 167.0 %collective-permute-start.4 = (f32[256,768]{1,0:T(8,128)}, f32[256,768]{1,0:T(8,128)S(1)}, u32[]{:S(2)}, u32[]{:S(2)}) collective-permute-start(f32[256,768]{1,0:T(8,128)} %get-tuple-element.9), channel_id=1, source_target_pairs={{0,16},{16,32},{32,48},{48,64},{64,80},{80,96},{96,112},{112,128},... | collective-permute-start | bytes 2359304 | tf_op jit(solution)/shard_map/ppermute | solution.py:26
  674.8 11.7 %collective-permute-start.5 = (f32[256,768]{1,0:T(8,128)S(1)}, f32[256,768]{1,0:T(8,128)}, u32[]{:S(2)}, u32[]{:S(2)}) collective-permute-start(f32[256,768]{1,0:T(8,128)S(1)} %get-tuple-element.10), channel_id=1, source_target_pairs={{0,16},{16,32},{32,48},{48,64},{64,80},{80,96},{96,112},{112,128},... | collective-permute-start | bytes 2359304 | tf_op jit(solution)/shard_map/ppermute | solution.py:26
  688.0 108.1 %collective-permute-start.6 = (f32[256,768]{1,0:T(8,128)S(1)}, f32[256,768]{1,0:T(8,128)S(1)}, u32[]{:S(2)}, u32[]{:S(2)}) collective-permute-start(f32[256,768]{1,0:T(8,128)S(1)} %get-tuple-element.4), channel_id=1, source_target_pairs={{0,464},{16,480},{32,496},{48,0},{64,16},{80,32},{96,48},{112,64},... | collective-permute-start | bytes 2359304 | tf_op jit(solution)/shard_map/ppermute | solution.py:26
  693.3 116.8 %collective-permute-start.7 = (f32[256,768]{1,0:T(8,128)S(1)}, f32[256,768]{1,0:T(8,128)S(1)}, u32[]{:S(2)}, u32[]{:S(2)}) collective-permute-start(f32[256,768]{1,0:T(8,128)S(1)} %get-tuple-element.6), channel_id=1, source_target_pairs={{0,464},{16,480},{32,496},{48,0},{64,16},{80,32},{96,48},{112,64},... | collective-permute-start | bytes 2359304 | tf_op jit(solution)/shard_map/ppermute | solution.py:26
Sparse Core Ops, SparseCore 0:
  14.3 164.7 all-gather.12
  181.8 144.0 all-gather.14
  328.0 161.2 all-gather.16
  491.8 175.5 all-gather.18
